TPU v7x, 128 devices: a whole 4x4x4 slice. The times are simulated.
128 devices in a mesh: blk: 32 (over z, x_lo, y), grp: 4 (over x_hi, core).
Axes of the slice: x: 4 (x_hi: 2, x_lo: 2; x = x_hi * 2 + x_lo), y: 4, z: 4, core: 2. Of those that a mesh axis runs over, the one named last changes fastest.
Arguments:
- acts: bfloat16 [1, 512, 256, 4096], P(None, 'blk', 'grp'), may hold values from -6 to 6
- out_grads: bfloat16 [1, 512, 256, 4096], P(None, 'blk', 'grp'), may hold values from -6 to 6
- proj_in: bfloat16 [1, 4096, 64], replicated, may hold values from -0.09375 to 0.09375
- proj_out: bfloat16 [1, 4096, 64], replicated, may hold values from -0.09375 to 0.09375
- lengths: int32 [512], P('blk'), may hold values from 1 to 256
- queries: bfloat16 [2048, 4096], P('blk'), may hold values from -0.09375 to 0.09375
Outputs:
- scores: float32 [512, 2048], P(('blk', 'grp'))
All inputs are finite; a program needn't handle non-finite values.
Results may differ from a plain program's by a relative error of at most 0.0049.
Values may be sent and summed in bfloat16 or wider, within the bound.
A program may use at most 128 MiB of HBM per device.

v0:
```python
import jax
import jax.numpy as jnp
from jax import lax
from jax.sharding import PartitionSpec as P


def project(rows, matrix):
    return jnp.einsum("lctd,ldr->lctr", rows, matrix, preferred_element_type=jnp.float32).astype(
        jnp.bfloat16
    )


def outer_sums(grad_side, input_side, lens):
    positions = jnp.arange(grad_side.shape[2], dtype=jnp.int32)
    masked = (positions[None, :] < lens[:, None]).astype(jnp.bfloat16)
    grad_masked = grad_side * masked[None, :, :, None]
    block = jnp.einsum(
        "lcta,lctb->clab", grad_masked, input_side, preferred_element_type=jnp.float32
    )
    return block.reshape(block.shape[0], -1)


def on_device(acts, out_grads, proj_in, proj_out, lengths, queries):
    group = lax.axis_index("grp")
    groups = lax.axis_size("grp")
    cand_blk = acts.shape[1]
    owned = cand_blk // groups
    stacked = jnp.concatenate([project(out_grads, proj_out), project(acts, proj_in)], axis=3)
    stacked = lax.all_to_all(stacked, "grp", split_axis=1, concat_axis=2, tiled=True)
    width = proj_in.shape[2]
    own_lens = lax.dynamic_slice_in_dim(lengths, group * owned, owned)
    grads = outer_sums(stacked[..., :width], stacked[..., width:], own_lens)
    scale = lax.rsqrt(jnp.mean(grads * grads, axis=1, keepdims=True) + 1e-06)
    unit = (grads * scale).astype(jnp.bfloat16)
    return lax.dot_general(
        unit,
        lax.all_gather(queries, "blk", axis=0, tiled=True),
        (((1,), (1,)), ((), ())),
        preferred_element_type=jnp.float32,
    )


def solution(mesh):
    in_specs = (
        P(None, "blk", "grp", None),
        P(None, "blk", "grp", None),
        P(),
        P(),
        P("blk"),
        P("blk", None),
    )
    out_specs = P(("blk", "grp"), None)
    return jax.shard_map(
        on_device, mesh=mesh, in_specs=in_specs, out_specs=out_specs, check_vma=False
    )
```

profile of v0, /device:TPU:0, one launch (start us, length us, event | category | flops | bytes accessed | tf_op | source)
XLA Modules:
  0.0 225.3 jit_solution(2176710123652143649)
XLA Ops:
  6.5 0.0 copy-start
  6.5 0.0 copy-start.2
  6.5 0.0 all-gather.2.cloned.1.call-start
  6.5 0.7 all-gather.2.cloned.1.call-update
  7.3 0.3 copy-done
  7.6 0.0 copy-start.1
  7.6 5.8 %fusion.10 = bf16[1,16,64,64]{3,2,1,0:T(8,128)(2,1)S(1)} fusion(bf16[1,16,64,4096]{3,2,1,0:T(8,128)(2,1)} %param.6, bf16[1,4096,64]{1,2,0:T(8,128)(2,1)S(1)} %copy-done), kind=kOutput, calls=%fused_computation.6 | convolution fusion | flops 536936448 | bytes 9043968 | tf_op jit(solution)/shard_map/lctd,ldr->lctr/dot_general | solution.py:8
  13.4 0.0 copy-done.2
  13.4 0.0 copy-done.1
  13.5 0.0 copy-start.3
  13.5 2.4 %fusion.13 = bf16[1,16,64,64]{3,2,1,0:T(8,128)(2,1)S(1)} fusion(bf16[1,16,64,4096]{3,2,1,0:T(8,128)(2,1)S(1)} %copy-done.1, bf16[1,4096,64]{1,2,0:T(8,128)(2,1)S(1)} %copy-done.2), kind=kOutput, calls=%fused_computation.7 | convolution fusion | flops 536936448 | bytes 9043968 | tf_op jit(solution)/shard_map/lctd,ldr->lctr/dot_general | solution.py:8
  15.8 0.9 maximum_bitcast_fusion
  16.7 4.4 %all-to-all-start = ((bf16[1,16,64,128]{3,2,0,1:T(8,128)(2,1)}), bf16[1,16,64,128]{3,2,0,1:T(8,128)(2,1)S(1)}, u32[]{:S(2)}, u32[]{:S(2)}) async-start(bf16[1,16,64,128]{3,2,0,1:T(8,128)(2,1)} %maximum_bitcast_fusion), calls=%async_computation | async-start | bytes 524288 | tf_op jit(solution)/shard_map/all_to_all | solution.py:29
  21.0 0.0 copy-done.3
  21.0 0.1 dynamic_slice.3
  21.1 0.1 fusion.24
  21.2 10.5 %all-to-all-done = bf16[1,16,64,128]{3,2,0,1:T(8,128)(2,1)S(1)} async-done(((bf16[1,16,64,128]{3,2,0,1:T(8,128)(2,1)}), bf16[1,16,64,128]{3,2,0,1:T(8,128)(2,1)S(1)}, u32[]{:S(2)}, u32[]{:S(2)}) %all-to-all-start) | async-done | bytes 262176 | tf_op jit(solution)/shard_map/all_to_all | solution.py:29
  31.7 0.6 multiply_reduce_fusion
  32.3 0.1 reshape.65
  32.4 175.2 %all-gather.2.cloned.1.call-done = bf16[2048,4096]{1,0:T(8,128)(2,1)} async-done(((bf16[64,4096]{1,0:T(8,128)(2,1)}), bf16[2048,4096]{1,0:T(8,128)(2,1)}) %all-gather.2.cloned.1.call-update) | async-done | bytes 16777232 | tf_op jit(solution)/shard_map/all_gather | solution.py:37
  207.6 10.8 %fusion.22 = f32[4,2048]{1,0:T(4,128)} fusion(bf16[2048,4096]{1,0:T(8,128)(2,1)} %all-gather.2.cloned.1.call-done, f32[4,4096]{1,0:T(4,128)S(1)} %reshape.65, f32[4]{0:T(128)S(1)} %add_rsqrt_fusion), kind=kOutput, calls=%fused_computation.18 | convolution fusion | flops 67141632 | bytes 16875536 | tf_op jit(solution)/shard_map/dot_general | solution.py:35
  (2 shorter events, 0.0 us)
Async XLA Ops:
  6.5 1.0 copy-start
  6.5 6.9 %copy-start.2 = (bf16[1,4096,64]{1,2,0:T(8,128)(2,1)S(1)}, bf16[1,4096,64]{1,2,0:T(8,128)(2,1)}, u32[]{:S(2)}) copy-start(bf16[1,4096,64]{1,2,0:T(8,128)(2,1)} %param.9) | copy-start | bytes 1572868
  6.5 201.1 %all-gather.2.cloned.1.call-start = ((), (), s32[]{:S(2)}) async-start(), calls=%async_computation.1 | async-start | bytes 17301504 | tf_op jit(solution)/shard_map/all_gather | solution.py:37
  7.6 5.9 %copy-start.1 = (bf16[1,16,64,4096]{3,2,1,0:T(8,128)(2,1)S(1)}, bf16[1,16,64,4096]{3,2,1,0:T(8,128)(2,1)}, u32[]{:S(2)}) copy-start(bf16[1,16,64,4096]{3,2,1,0:T(8,128)(2,1)} %param.7) | copy-start | bytes 25165828
  13.5 7.6 %copy-start.3 = (s32[16]{0:T(128)S(1)}, s32[16]{0:T(128)}, u32[]{:S(2)}) copy-start(s32[16]{0:T(128)} %param.10) | copy-start | bytes 196
  16.7 15.0 %all-to-all-start = ((bf16[1,16,64,128]{3,2,0,1:T(8,128)(2,1)}), bf16[1,16,64,128]{3,2,0,1:T(8,128)(2,1)S(1)}, u32[]{:S(2)}, u32[]{:S(2)}) async-start(bf16[1,16,64,128]{3,2,0,1:T(8,128)(2,1)} %maximum_bitcast_fusion), calls=%async_computation | async-start | bytes 524288 | tf_op jit(solution)/shard_map/all_to_all | solution.py:29
Sparse Core Ops, SparseCore 0:
  9.0 198.5 all-gather.1
where the time goes:
time: 226 us; the launch traced here: 225 us
  waiting for transfers between devices  186 us (82%)
  matrix products  19.6 us (9%)
  between operations  13.4 us (6%)
  starting transfers between devices  4.37 us (2%)
    all_gather x1, waiting for transfers between devices, on_device(): lax.all_gather(queries, 'blk', axis=0, tiled=True)  175 us
    dot_general x1, matrix products, on_device(): lax.dot_general(unit, lax.all_gather(queries, 'blk', axis=0, tiled=True),...  10.8 us
    all_to_all x1, waiting for transfers between devices, on_device(): lax.all_to_all(stacked, 'grp', split_axis=1, concat_axis=2, tiled=True)  10.5 us
    dot_general x2, matrix products, project(): jnp.einsum('lctd,ldr->lctr', rows, matrix, preferred_element_type=jnp.flo...  8.2 us
  transfers between devices with their start and end apart: 2, of which 2 were waited for; matrix products, arithmetic and copies ran while one was open for 4% of the time, Pallas kernels for 0%

commit v1 on v0

--- a/solution.py
+++ b/solution.py
@@ -2,6 +2,12 @@
 import jax.numpy as jnp
 from jax import lax
 from jax.sharding import PartitionSpec as P
+
+
+def pairs_all_touch(local_array):
+    return jnp.concatenate(
+        lax.all_to_all(jnp.stack([local_array] * lax.axis_size("blk")), "blk", 0, 0), axis=0
+    )
 
 
 def project(rows, matrix):
@@ -33,10 +39,7 @@
     scale = lax.rsqrt(jnp.mean(grads * grads, axis=1, keepdims=True) + 1e-06)
     unit = (grads * scale).astype(jnp.bfloat16)
     return lax.dot_general(
-        unit,
-        lax.all_gather(queries, "blk", axis=0, tiled=True),
-        (((1,), (1,)), ((), ())),
-        preferred_element_type=jnp.float32,
+        unit, pairs_all_touch(queries), (((1,), (1,)), ((), ())), preferred_element_type=jnp.float32
     )
 
 

time: 226 us -> 385 us (1.70)
  the two profiles are of different devices: /device:TPU:0 before, /device:TPU:8 now
where the time goes in v1:
time: 385 us
  waiting for transfers between devices  337 us (88%)
  matrix products  19.8 us (5%)
  blocking collectives  11.6 us (3%)
  starting transfers between devices  8.77 us (2%)
  local copies, waits for them, and re-layouts  7.14 us (2%)
    all_to_all x1, waiting for transfers between devices, pairs_all_touch(): lax.all_to_all(jnp.stack([local_array] * lax.axis_size('blk')), 'blk', 0, 0)  337 us
    all_to_all x1, blocking collectives, on_device(): lax.all_to_all(stacked, 'grp', split_axis=1, concat_axis=2, tiled=True)  11.6 us
    dot_general x1, matrix products, on_device(): lax.dot_general(unit, pairs_all_touch(queries), (((1,), (1,)), ((), ())),...  10.8 us
    all_to_all x1, starting transfers between devices, pairs_all_touch(): lax.all_to_all(jnp.stack([local_array] * lax.axis_size('blk')), 'blk', 0, 0)  8.77 us
    dot_general x2, matrix products, project(): jnp.einsum('lctd,ldr->lctr', rows, matrix, preferred_element_type=jnp.flo...  8.46 us
  transfers between devices with their start and end apart: 1, of which 1 were waited for; matrix products, arithmetic and copies ran while one was open for 0% of the time, Pallas kernels for 0%

profile of v1, /device:TPU:8, one launch (start us, length us, event | category | flops | bytes accessed | tf_op | source)
XLA Modules:
  0.0 384.6 jit_solution(11900119224105218818)
XLA Ops:
  0.0 0.0 copy-start
  0.0 0.0 copy-start.3
  0.0 0.0 copy-start.2
  0.0 1.0 copy-done
  1.0 6.1 %fusion.10 = bf16[1,16,64,64]{3,2,1,0:T(8,128)(2,1)S(1)} fusion(bf16[1,16,64,4096]{3,2,1,0:T(8,128)(2,1)} %param.6, bf16[1,4096,64]{1,2,0:T(8,128)(2,1)S(1)} %copy-done), kind=kOutput, calls=%fused_computation.6 | convolution fusion | flops 536936448 | bytes 9043968 | tf_op jit(solution)/shard_map/lctd,ldr->lctr/dot_general | solution.py:14
  7.2 0.0 copy-done.3
  7.2 0.0 copy-done.2
  7.2 0.0 copy-start.1
  7.2 2.3 fusion.13
  9.5 0.2 maximum_bitcast_fusion
  9.7 11.6 %all_to_all.23 = bf16[1,16,64,128]{3,2,0,1:T(8,128)(2,1)S(1)} all-to-all(bf16[1,16,64,128]{3,2,0,1:T(8,128)(2,1)S(1)} %maximum_bitcast_fusion), channel_id=1, replica_groups=mesh['blk'=32,'grp'=4] {'grp'}, dimensions={1} | all-to-all | bytes 524288 | tf_op jit(solution)/shard_map/all_to_all | solution.py:35
  21.3 0.0 copy-done.1
  21.3 5.9 %stack.2 = bf16[32,64,4096]{2,1,0:T(8,128)(2,1)} broadcast(bf16[64,4096]{1,0:T(8,128)(2,1)S(1)} %copy-done.1), dimensions={1,2} | broadcast | bytes 17301504 | tf_op jit(solution)/shard_map/stack | solution.py:9
  27.2 0.0 copy-start.4
  27.2 8.8 %all-to-all-start.1 = ((bf16[32,64,4096]{2,1,0:T(8,128)(2,1)}), bf16[32,64,4096]{2,1,0:T(8,128)(2,1)}, u32[]{:S(2)}, u32[]{:S(2)}) async-start(bf16[32,64,4096]{2,1,0:T(8,128)(2,1)} %stack.2), calls=%async_computation.1 | async-start | bytes 33554432 | tf_op jit(solution)/shard_map/all_to_all | solution.py:9
  36.0 0.0 copy-done.4
  36.0 0.1 dynamic_slice.3
  36.1 0.1 fusion.22
  36.2 0.6 multiply_reduce_fusion
  36.8 0.1 multiply_convert_fusion
  36.9 0.1 convert_element_type.31
  37.0 336.8 %all-to-all-done.1 = bf16[32,64,4096]{2,1,0:T(8,128)(2,1)} async-done(((bf16[32,64,4096]{2,1,0:T(8,128)(2,1)}), bf16[32,64,4096]{2,1,0:T(8,128)(2,1)}, u32[]{:S(2)}, u32[]{:S(2)}) %all-to-all-start.1) | async-done | bytes 16777248 | tf_op jit(solution)/shard_map/all_to_all | solution.py:9
  373.8 10.8 %fusion.23 = f32[4,2048]{1,0:T(4,128)} fusion(bf16[4,4096]{1,0:T(4,128)(2,1)S(1)} %convert_element_type.31, bf16[2048,4096]{1,0:T(8,128)(2,1)} %bitcast.14), kind=kOutput, calls=%fused_computation.21 | convolution fusion | flops 67108864 | bytes 16842752 | tf_op jit(solution)/shard_map/dot_general | solution.py:41
  (2 shorter events, 0.0 us)
Async XLA Ops:
  0.0 1.0 copy-start
  0.0 7.2 %copy-start.3 = (bf16[1,4096,64]{1,2,0:T(8,128)(2,1)S(1)}, bf16[1,4096,64]{1,2,0:T(8,128)(2,1)}, u32[]{:S(2)}) copy-start(bf16[1,4096,64]{1,2,0:T(8,128)(2,1)} %param.9) | copy-start | bytes 1572868
  0.0 7.2 %copy-start.2 = (bf16[1,16,64,4096]{3,2,1,0:T(8,128)(2,1)S(1)}, bf16[1,16,64,4096]{3,2,1,0:T(8,128)(2,1)}, u32[]{:S(2)}) copy-start(bf16[1,16,64,4096]{3,2,1,0:T(8,128)(2,1)} %param.7) | copy-start | bytes 25165828
  7.2 14.1 %copy-start.1 = (bf16[64,4096]{1,0:T(8,128)(2,1)S(1)}, bf16[64,4096]{1,0:T(8,128)(2,1)}, u32[]{:S(2)}) copy-start(bf16[64,4096]{1,0:T(8,128)(2,1)} %param.11) | copy-start | bytes 1572868
  27.2 8.8 %copy-start.4 = (s32[16]{0:T(128)S(1)}, s32[16]{0:T(128)}, u32[]{:S(2)}) copy-start(s32[16]{0:T(128)} %param.10) | copy-start | bytes 196
  27.2 346.6 %all-to-all-start.1 = ((bf16[32,64,4096]{2,1,0:T(8,128)(2,1)}), bf16[32,64,4096]{2,1,0:T(8,128)(2,1)}, u32[]{:S(2)}, u32[]{:S(2)}) async-start(bf16[32,64,4096]{2,1,0:T(8,128)(2,1)} %stack.2), calls=%async_computation.1 | async-start | bytes 33554432 | tf_op jit(solution)/shard_map/all_to_all | solution.py:9
